TPU v7x, 1024 devices: a whole 4x8x16 slice. The times are simulated.
1024 devices in a mesh: group: 16 (over z), expert: 64 (over x, y, core).
Axes of the slice: x: 4, y: 8, z: 16, core: 2. Of those that a mesh axis runs over, the one named last changes fastest.
Arguments:
- tokens: bfloat16 [16384, 3584], P(('group', 'expert')), parts along dimension 0, may hold values from -6 to 6
- w_in: bfloat16 [2, 3584, 131072], P(None, None, ('group', 'expert')), parts along dimension 2, may hold values from -0.09375 to 0.09375
- w_down: bfloat16 [131072, 3584], P(('group', 'expert')), parts along dimension 0, may hold values from -0.1875 to 0.1875
- old_place: int32 [128], P('group'), parts along dimension 0, may hold values from 0 to 5, as said below
- new_place: int32 [128], P('group'), parts along dimension 0, may hold values from 0 to 5, as said below
- expert_ids: int32 [16384, 2], P(('group', 'expert')), parts along dimension 0, may hold values from 0 to 5, all different within a row
- replica: int32 [16384, 2], P(('group', 'expert')), parts along dimension 0, may hold values from 0 to 1
- combine: float32 [16384, 2], P(('group', 'expert')), parts along dimension 0, may hold values from 0.2 to 1
Outputs:
- mixed: bfloat16 [16384, 3584], P(('group', 'expert')), parts along dimension 0
There are 16 independent parts, one for each index of `group`. A program takes and returns all parts, laid end to end along the dimension named above; each array names one. Nothing has to cross between parts.
Inputs may be any that keep to these rules, and one draw needn't show every extreme that they name: Each of the 6 experts is held by one or two slots of old_place; exactly two experts are held twice. new_place is old_place with the entries of some pairs of slots 2 i and 2 i + 1 exchanged.
All inputs are finite; a program needn't handle non-finite values.
Results may differ from a plain program's by a relative error of at most 0.0057.
Values may be sent and summed in bfloat16 or wider, within the bound.
A program may use at most 32 MiB of HBM per device.

v0:
```python
import jax
import jax.numpy as jnp
from jax import lax
from jax.sharding import PartitionSpec as P

SLOTS = 8
EXPERTS = 6
CAP = 4


def routing(new_place, expert_ids, replica):
    slot_ids = jnp.arange(SLOTS, dtype=jnp.int32)
    experts = jnp.arange(EXPERTS, dtype=jnp.int32)
    holders = (new_place[None, :] == experts[:, None]).astype(jnp.int32)
    counts = jnp.sum(holders, axis=1)
    before = jnp.cumsum(holders, axis=1) - holders
    expert_hot = (expert_ids[..., None] == experts).astype(jnp.int32)
    count_sel = jnp.sum(expert_hot * counts, axis=-1)
    wanted = replica % jnp.maximum(count_sel, 1)
    holder_sel = jnp.sum(expert_hot[..., None] * holders, axis=2)
    rank_sel = jnp.sum(expert_hot[..., None] * before, axis=2)
    chosen = holder_sel * (rank_sel == wanted[..., None]).astype(jnp.int32)
    return (chosen, jnp.sum(chosen * slot_ids, axis=-1))


def body(tokens, w_in, w_down, old_place, new_place, expert_ids, replica, combine):
    devices = lax.axis_size("expert")
    shards = devices // SLOTS
    model_width = tokens.shape[1]
    slot_ids = jnp.arange(SLOTS, dtype=jnp.int32)
    source = jnp.where(new_place == old_place, slot_ids, slot_ids + 1 - 2 * (slot_ids % 2))
    chosen, dest_slot = routing(new_place, expert_ids, replica)
    flat_chosen = chosen.reshape(-1, SLOTS)
    position = (jnp.cumsum(flat_chosen, axis=0) - flat_chosen).reshape(chosen.shape)
    position = jnp.sum(chosen * position, axis=-1)
    is_kept = position < CAP
    target = jnp.where(is_kept, dest_slot * CAP + position, -1)
    columns = jnp.arange(SLOTS * CAP, dtype=jnp.int32)
    matches = target[..., None] == columns
    selector = jnp.sum(matches.astype(jnp.int32), axis=1).astype(jnp.bfloat16)
    combiner = jnp.sum(combine[..., None] * matches.astype(jnp.float32), axis=1)
    buffer = jnp.einsum("rj,rd->jd", selector, tokens, preferred_element_type=jnp.float32)
    buffer = buffer.astype(jnp.bfloat16).reshape(SLOTS, CAP, model_width)
    ordered = jnp.take(buffer, source, axis=0)
    blocks = jnp.broadcast_to(ordered[:, None], (SLOTS, shards, CAP, model_width)).reshape(
        devices, CAP, model_width
    )
    received = lax.all_to_all(blocks, "expert", split_axis=0, concat_axis=0, tiled=True)
    flat_rows = received.reshape(-1, model_width)
    gate_up = jnp.einsum("rd,gdh->grh", flat_rows, w_in, preferred_element_type=jnp.float32)
    hidden = (jax.nn.silu(gate_up[0]) * gate_up[1]).astype(jnp.bfloat16)
    partial_value = jnp.dot(hidden, w_down, preferred_element_type=jnp.float32).astype(jnp.bfloat16)
    returned = lax.all_to_all(
        partial_value.reshape(received.shape), "expert", split_axis=0, concat_axis=0, tiled=True
    )
    returned = returned.reshape(SLOTS, shards, CAP, model_width)
    returned = jnp.take(returned, source, axis=0)
    summed = jnp.sum(returned.astype(jnp.float32), axis=1).reshape(SLOTS * CAP, model_width)
    mixed = jnp.dot(
        combiner, summed, precision=lax.Precision.HIGHEST, preferred_element_type=jnp.float32
    )
    return mixed.astype(jnp.bfloat16)


def solution(mesh):
    placed = (
        P(("group", "expert"), None),
        P(None, None, ("group", "expert")),
        P(("group", "expert"), None),
        P("group"),
        P("group"),
        P(("group", "expert"), None),
        P(("group", "expert"), None),
        P(("group", "expert"), None),
    )
    return jax.shard_map(
        body, mesh=mesh, in_specs=placed, out_specs=P(("group", "expert"), None), check_vma=False
    )
```

profile of v0, /device:TPU:1, one launch (start us, length us, event | category | flops | bytes accessed | tf_op | source)
XLA Modules:
  0.0 143.9 jit_solution(12932119866132340029)
XLA Ops:
  0.0 0.8 fusion.7
  0.8 0.2 reduce_window_sum.24
  1.0 0.8 fusion.8
  1.7 0.7 fusion.5
  2.7 0.8 select_reduce_fusion.1
  3.4 0.8 and_select_fusion.1
  4.2 0.1 copy.22
  4.3 0.1 eq.93
  4.7 1.1 convolution_convert_fusion.1
  5.9 0.7 compare_and_fusion
  6.6 0.7 gather_fusion
  7.4 0.2 broadcast_select_fusion
  7.6 0.5 broadcast_in_dim.53
  8.0 63.5 %all_to_all.10 = bf16[64,4,3584]{2,1,0:T(4,128)(2,1)} all-to-all(bf16[64,4,3584]{2,1,0:T(4,128)(2,1)S(1)} %bitcast.25), channel_id=1, replica_groups=mesh['group'=16,'expert'=64] {'expert'}, dimensions={0} | all-to-all | bytes 3670016 | tf_op jit(solution)/shard_map/all_to_all | solution.py:48
  71.5 3.9 %reshape.172 = bf16[256,3584,1]{1,0,2:T(8,128)(2,1)} reshape(bf16[64,4,3584]{2,1,0:T(4,128)(2,1)} %all_to_all.10) | data formatting | bytes 3670016 | tf_op jit(solution)/shard_map/reshape | solution.py:49
  75.5 2.2 %convolution_bitcast_fusion = f32[2,256,128]{2,1,0:T(8,128)S(1)} fusion(bf16[256,3584,1]{1,0,2:T(8,128)(2,1)} %reshape.172, bf16[2,3584,128]{2,1,0:T(8,128)(2,1)S(1)} %copy-done), kind=kOutput, calls=%fused_computation.6 | convolution fusion | flops 469762048 | bytes 3932160 | tf_op jit(solution)/shard_map/rd,gdh->grh/dot_general | solution.py:50
  77.7 1.9 %convolution_convert_fusion = bf16[256,3584]{1,0:T(8,128)(2,1)} fusion(bf16[128,3584]{1,0:T(8,128)(2,1)S(1)} %copy-done.1, f32[2,256,128]{2,1,0:T(8,128)S(1)} %convolution_bitcast_fusion), kind=kOutput, calls=%fused_computation.2 | convolution fusion | flops 235995136 | bytes 3014656 | tf_op jit(solution)/shard_map/dot_general | solution.py:52
  79.6 4.1 %reshape.151 = bf16[64,4,3584]{2,1,0:T(4,128)(2,1)} reshape(bf16[256,3584]{1,0:T(8,128)(2,1)} %convolution_convert_fusion) | data formatting | bytes 3670016 | tf_op jit(solution)/shard_map/reshape | solution.py:54
  83.6 6.3 %all-to-all-start.1 = ((bf16[64,4,3584]{2,1,0:T(4,128)(2,1)}), bf16[64,4,3584]{2,1,0:T(4,128)(2,1)}, u32[]{:S(2)}, u32[]{:S(2)}) async-start(bf16[64,4,3584]{2,1,0:T(4,128)(2,1)} %reshape.151), calls=%async_computation.1 | async-start | bytes 3670016 | tf_op jit(solution)/shard_map/all_to_all | solution.py:53
  90.1 45.2 %all-to-all-done.1 = bf16[64,4,3584]{2,1,0:T(4,128)(2,1)} async-done(((bf16[64,4,3584]{2,1,0:T(4,128)(2,1)}), bf16[64,4,3584]{2,1,0:T(4,128)(2,1)}, u32[]{:S(2)}, u32[]{:S(2)}) %all-to-all-start.1) | async-done | bytes 1835040 | tf_op jit(solution)/shard_map/all_to_all | solution.py:53
  135.3 4.7 %gather_fusion.1 = bf16[8,8,4,3584]{3,2,1,0:T(4,128)(2,1)} fusion(bf16[8,8,4,3584]{3,2,1,0:T(4,128)(2,1)} %bitcast.7, s32[1024]{0:T(1024)S(1)} %pad_clamp_fusion), kind=kCustom, calls=%fused_computation.1 | custom fusion | bytes 3670048 | tf_op jit(solution)/shard_map/jit(_take)/gather | solution.py:57
  140.0 2.7 %convert_reduce_fusion = f32[8,4,3584]{2,1,0:T(4,128)S(1)} fusion(bf16[8,8,4,3584]{3,2,1,0:T(4,128)(2,1)} %gather_fusion.1, pred[8]{0:T(512)(128)(4,1)S(1)} %get-tuple-element.9), kind=kLoop, calls=%fused_computation.5 | loop fusion | flops 2637824 | bytes 2293768 | tf_op jit(solution)/shard_map/reduce_sum | solution.py:58
  142.7 0.2 reshape.153
  142.9 1.0 convolution_convert_fusion.2
  (19 shorter events, 0.7 us)
Async XLA Ops:
  0.0 75.5 %copy-start = (bf16[2,3584,128]{2,1,0:T(8,128)(2,1)S(1)}, bf16[2,3584,128]{2,1,0:T(8,128)(2,1)}, u32[]{:S(2)}) copy-start(bf16[2,3584,128]{2,1,0:T(8,128)(2,1)} %param.9) | copy-start | bytes 5505028
  75.5 2.2 %copy-start.1 = (bf16[128,3584]{1,0:T(8,128)(2,1)S(1)}, bf16[128,3584]{1,0:T(8,128)(2,1)}, u32[]{:S(2)}) copy-start(bf16[128,3584]{1,0:T(8,128)(2,1)} %param.10) | copy-start | bytes 2752516
  83.6 6.3 %copy-start.2 = (f32[16,2]{0,1:T(2,128)S(1)}, f32[16,2]{0,1:T(2,128)}, u32[]{:S(2)}) copy-start(f32[16,2]{0,1:T(2,128)} %param.15) | copy-start | bytes 388
  83.6 51.7 %all-to-all-start.1 = ((bf16[64,4,3584]{2,1,0:T(4,128)(2,1)}), bf16[64,4,3584]{2,1,0:T(4,128)(2,1)}, u32[]{:S(2)}, u32[]{:S(2)}) async-start(bf16[64,4,3584]{2,1,0:T(4,128)(2,1)} %reshape.151), calls=%async_computation.1 | async-start | bytes 3670016 | tf_op jit(solution)/shard_map/all_to_all | solution.py:53
where the time goes:
time: 145 us; the launch traced here: 144 us
  blocking collectives  63.5 us (44%)
  waiting for transfers between devices  45.2 us (31%)
  local copies, waits for them, and re-layouts  14.6 us (10%)
  other arithmetic  7.92 us (5%)
  starting transfers between devices  6.33 us (4%)
  matrix products  6.24 us (4%)
    all_to_all x1, blocking collectives, body(): lax.all_to_all(blocks, 'expert', split_axis=0, concat_axis=0, tiled=True)  63.5 us
    all_to_all x1, waiting for transfers between devices, body(): lax.all_to_all(partial_value.reshape(received.shape), 'expert', split_axi...  45.2 us
    all_to_all x1, starting transfers between devices, body(): lax.all_to_all(partial_value.reshape(received.shape), 'expert', split_axi...  6.33 us
    gather x1, local copies, waits for them, and re-layouts, body(): returned = jnp.take(returned, source, axis=0)  4.74 us
    reshape x1, local copies, waits for them, and re-layouts, body(): partial_value.reshape(received.shape)  4.06 us
    reshape x1, local copies, waits for them, and re-layouts, body(): flat_rows = received.reshape(-1, model_width)  3.91 us
  transfers between devices with their start and end apart: 1, of which 1 were waited for; matrix products, arithmetic and copies ran while one was open for 0% of the time, Pallas kernels for 0%

commit v1 on v0

v1 whole, which is shorter than its diff:
```python
import functools

import jax
import jax.numpy as jnp
from jax import lax
from jax.experimental import pallas as pl
from jax.experimental.pallas import tpu as pltpu
from jax.sharding import PartitionSpec as P

SLOTS = 8
CAP = 4
NX, NY = 4, 8
META = 128
TILE = 512
F32 = jnp.float32
BF16 = jnp.bfloat16


def routing_meta(old_place, new_place, expert_ids, replica, combine):
    rows = expert_ids.shape[0]
    lane = lax.broadcasted_iota(jnp.int32, (1, META), 1)
    new_vec = jnp.full((1, META), -1, jnp.int32)
    old_vec = jnp.full((1, META), -1, jnp.int32)
    for t in range(SLOTS):
        new_vec = jnp.where(lane == t, new_place[t], new_vec)
        old_vec = jnp.where(lane == t, old_place[t], old_vec)
    count = jnp.zeros((1, META), jnp.int32)
    rank = jnp.zeros((1, META), jnp.int32)
    for t in range(SLOTS):
        same = jnp.where(new_vec == new_place[t], 1, 0)
        count = count + same
        rank = rank + jnp.where(lane > t, same, 0)
    source = jnp.where(new_vec == old_vec, lane, lane + 1 - 2 * (lane & 1))
    chosen = []
    for k in range(2):
        wanted = replica[:, k:k + 1]
        wanted = jnp.where(wanted < count, wanted, wanted - count)
        hit = (new_vec == expert_ids[:, k:k + 1]) & (rank == wanted)
        chosen.append(jnp.where(hit, 1.0, 0.0))
    row_i = lax.broadcasted_iota(jnp.int32, (rows, rows), 0)
    col_i = lax.broadcasted_iota(jnp.int32, (rows, rows), 1)
    earlier = jnp.where(col_i < row_i, 1.0, 0.0).astype(BF16)
    before = jnp.dot(earlier, (chosen[0] + chosen[1]).astype(BF16), preferred_element_type=F32)
    lanes = lax.broadcasted_iota(jnp.int32, (rows, META), 1)
    column = (lanes & 31).astype(F32)
    block = lanes >> 5
    source_f = (source * CAP).astype(F32)
    meta = jnp.zeros((rows, META), F32)
    for k in range(2):
        ahead = before if k == 0 else before + chosen[0]
        position = jnp.sum(chosen[k] * ahead, axis=1, keepdims=True)
        target = jnp.sum(chosen[k] * source_f, axis=1, keepdims=True) + position
        weight = combine[:, k:k + 1]
        high = weight.astype(BF16).astype(F32)
        middle = (weight - high).astype(BF16).astype(F32)
        low = weight - high - middle
        value = jnp.where(block == 0, high, jnp.where(block == 1, middle, jnp.where(block == 2, low, 1.0)))
        meta = meta + jnp.where((column == target) & (position < float(CAP)), value, 0.0)
    return meta.astype(BF16)


def kernel(tokens, w_in, w_down, old_place, new_place, expert_ids, replica, combine, out,
           units, sel, rows, w_gu, w_d, p_send, p_recv, p_own, r_send, r_recv, part, y_send, y_recv,
           ssem, rsem, wsem):
    width = tokens.shape[1]
    hid = w_down.shape[0]
    me = lax.axis_index("expert")
    core = me % 2
    y = (me // 2) % NY
    x = me // (2 * NY)
    half = y // (NY // 2)

    def device(xx, yy, cc):
        return {"expert": (xx * NY + yy) * 2 + cc}

    up = device(x, (y + 1) % NY, core)
    down = device(x, (y + NY - 1) % NY, core)
    partner = device(x, y, 1 - core)
    right = [device((x + d) % NX, y, core) for d in range(NX)]
    left = [device((x + NX - d) % NX, y, core) for d in range(NX)]

    barrier = pltpu.get_barrier_semaphore()
    peers = [up, down, partner] + right[1:]
    for peer in peers:
        pl.semaphore_signal(barrier, inc=1, device_id=peer, device_id_type=pl.DeviceIdType.MESH)

    loads = [
        pltpu.make_async_copy(w_in.at[0], w_gu.at[:, 0:hid], wsem.at[0]),
        pltpu.make_async_copy(w_in.at[1], w_gu.at[:, hid:2 * hid], wsem.at[1]),
        pltpu.make_async_copy(w_down, w_d, wsem.at[2]),
    ]
    for load in loads:
        load.start()

    units[0, :, META:] = tokens[...]
    units[0, :, :META] = routing_meta(old_place, new_place, expert_ids[...], replica[...], combine[...])
    pl.semaphore_wait(barrier, len(peers))

    sent = []

    def push(src, dst, target):
        i = len(sent)
        copy = pltpu.make_async_remote_copy(
            src_ref=src, dst_ref=dst, send_sem=ssem.at[i], recv_sem=rsem.at[i],
            device_id=target, device_id_type=pl.DeviceIdType.MESH)
        copy.start()
        sent.append(copy)
        return copy

    cuts = (pl.ds(0, 1920), pl.ds(1920, 1792))

    def forward(src, dst, target, c):
        return push(units.at[src, :, cuts[c]], units.at[dst, :, cuts[c]], target)

    a1 = [(forward(0, 1, up, c), forward(0, 2, down, c)) for c in range(2)]
    a2 = []
    for c in range(2):
        a1[c][0].wait_recv()
        u = forward(1, 3, up, c)
        a1[c][1].wait_recv()
        a2.append((u, forward(2, 4, down, c)))
    a3 = []
    for c in range(2):
        a2[c][0].wait_recv()
        u = forward(3, 5, up, c)
        a2[c][1].wait_recv()
        a3.append((u, forward(4, 6, down, c)))

    lane_i = lax.broadcasted_iota(jnp.int32, (META, 4 * META), 0)
    n_i = lax.broadcasted_iota(jnp.int32, (META, 4 * META), 1)
    n_in = n_i & (META - 1)
    wanted = 32 * (n_i >> 7) + 8 * ((x + (n_in >> 4)) & (NX - 1)) + CAP * half + (n_in & 3)
    spread = jnp.where((lane_i == wanted) & (n_in < 64), 1.0, 0.0).astype(BF16)
    u_row = lax.broadcasted_iota(jnp.int32, (64, 64), 0) >> 4
    u_col = (lax.broadcasted_iota(jnp.int32, (64, 64), 1) >> 2) & 3
    same_unit = u_row == u_col

    def select(g):
        meta = units[4 * g:4 * g + 4, :, :META].reshape(64, META)
        picks = jnp.dot(meta, spread, preferred_element_type=F32)
        mats = [jnp.where(same_unit, picks[:, q * META:q * META + 64], 0.0).astype(BF16) for q in range(4)]
        for j in range(width // TILE):
            group = units[4 * g:4 * g + 4, :, META + j * TILE:META + (j + 1) * TILE].reshape(64, TILE)
            got = lax.dot_general(mats[3], group, (((0,), (0,)), ((), ())), preferred_element_type=F32)
            got = got.astype(BF16)
            rows[g, 0, 0, :, j * TILE:(j + 1) * TILE] = got[0:16]
            for d in range(1, NX):
                sel[g, d, :, j * TILE:(j + 1) * TILE] = got[16 * d:16 * d + 16]
        weights = jnp.concatenate(mats[:3], axis=0)
        copies = [None] + [push(sel.at[g, d], rows.at[g, 0, d], right[d]) for d in range(1, NX)]
        return weights, copies

    def swap(g, d):
        return push(rows.at[g, 0, d], rows.at[g, 1, d], partner)

    def experts(g):
        block = rows[g].reshape(2 * 64, width)
        gate_up = jnp.dot(block, w_gu[...], preferred_element_type=F32)
        gate = gate_up[:, :hid]
        hidden = (gate * jax.nn.sigmoid(gate) * gate_up[:, hid:]).astype(BF16)
        for j in range(width // TILE):
            cut = slice(j * TILE, (j + 1) * TILE)
            value = jnp.dot(hidden, w_d[:, cut], preferred_element_type=F32)
            p_own[g, :, cut] = value[:64]
            p_send[g, :, cut] = value[64:].astype(BF16)
        return push(p_send.at[g], p_recv.at[g], partner)

    def give_back(g, copy):
        copy.wait_recv()
        for d in range(NX):
            total = p_own[g, 16 * d:16 * d + 16] + p_recv[g, 16 * d:16 * d + 16].astype(F32)
            if d == 0:
                r_recv[g, 0:16] = total.astype(BF16)
            else:
                r_send[g, 16 * d:16 * d + 16] = total.astype(BF16)
        return [push(r_send.at[g, pl.ds(16 * d, 16)], r_recv.at[g, pl.ds(16 * d, 16)], left[d])
                for d in range(1, NX)]

    def mix(g, weights, copies):
        for copy in copies:
            copy.wait_recv()
        for j in range(width // TILE):
            cut = slice(j * TILE, (j + 1) * TILE)
            value = jnp.dot(weights, r_recv[g, :, cut], preferred_element_type=F32)
            value = value[0:64] + value[64:128] + value[128:192]
            part[4 * g:4 * g + 4, :, cut] = value.reshape(4, 16, TILE)

    weights_a, x_a = select(0)
    a4 = []
    for c in range(2):
        a3[c][0].wait_recv()
        if c == 0:
            a4.append(forward(5, 7, up, 0))
        a3[c][1].wait_recv()
        if c == 1:
            a4.append(forward(6, 7, down, 1))
    s_a = [swap(0, 0)]
    for copy in a4:
        copy.wait_recv()
    weights_b, x_b = select(1)
    s_b = [swap(1, 0)]
    for d in range(1, NX):
        x_a[d].wait_recv()
        s_a.append(swap(0, d))
    for load in loads:
        load.wait()
    for copy in s_a:
        copy.wait_recv()
    p_a = experts(0)
    for d in range(1, NX):
        x_b[d].wait_recv()
        s_b.append(swap(1, d))
    r_a = give_back(0, p_a)
    for copy in s_b:
        copy.wait_recv()
    p_b = experts(1)
    r_b = give_back(1, p_b)
    mix(0, weights_a, r_a)
    mix(1, weights_b, r_b)

    halves = (slice(0, width // 2), slice(width // 2, width))

    def hand(k, dst, c, target, arrived):
        value = part[k, :, halves[c]]
        if arrived is not None:
            arrived.wait_recv()
            value = value + y_recv[k, :, halves[c]].astype(F32)
        y_send[k, :, halves[c]] = value.astype(BF16)
        cut = pl.ds(c * (width // 2), width // 2)
        return push(y_send.at[k, :, cut], y_recv.at[dst, :, cut], target)

    got_down = {0: hand(7, 5, 0, down, None), 1: None}
    got_up = {0: None, 1: hand(7, 6, 1, up, None)}
    for k_down, d_down, k_up, d_up in ((5, 3, 6, 4), (3, 1, 4, 2), (1, 0, 2, 7)):
        next_down, next_up = {}, {}
        for c in range(2):
            order = (1 - c) if k_down == 5 else c
            next_down[order] = hand(k_down, d_down, order, down, got_down[order])
            other = c
            next_up[other] = hand(k_up, d_up, other, up, got_up[other])
        got_down, got_up = next_down, next_up
    for c in range(2):
        got_down[c].wait_recv()
        got_up[c].wait_recv()
        value = (part[0, :, halves[c]] + y_recv[0, :, halves[c]].astype(F32)
                 + y_recv[7, :, halves[c]].astype(F32))
        out[:, halves[c]] = value.astype(BF16)
    for copy in sent:
        copy.wait_send()


COPIES = 14 + 6 + 8 + 2 + 6 + 14


def body(tokens, w_in, w_down, old_place, new_place, expert_ids, replica, combine):
    count, width = tokens.shape
    hid = w_down.shape[0]
    vmem = pl.BlockSpec(memory_space=pltpu.VMEM)
    smem = pl.BlockSpec(memory_space=pltpu.SMEM)
    hbm = pl.BlockSpec(memory_space=pl.ANY)
    return pl.pallas_call(
        kernel,
        out_shape=jax.ShapeDtypeStruct((count, width), BF16),
        in_specs=[vmem, hbm, hbm, smem, smem, vmem, vmem, vmem],
        out_specs=vmem,
        scratch_shapes=[
            pltpu.VMEM((8, count, META + width), BF16),
            pltpu.VMEM((2, NX, 16, width), BF16),
            pltpu.VMEM((2, 2, NX, 16, width), BF16),
            pltpu.VMEM((width, 2 * hid), BF16),
            pltpu.VMEM((hid, width), BF16),
            pltpu.VMEM((2, 64, width), BF16),
            pltpu.VMEM((2, 64, width), BF16),
            pltpu.VMEM((2, 64, width), F32),
            pltpu.VMEM((2, 64, width), BF16),
            pltpu.VMEM((2, 64, width), BF16),
            pltpu.VMEM((8, count, width), F32),
            pltpu.VMEM((8, count, width), BF16),
            pltpu.VMEM((8, count, width), BF16),
            pltpu.SemaphoreType.DMA((COPIES,)),
            pltpu.SemaphoreType.DMA((COPIES,)),
            pltpu.SemaphoreType.DMA((3,)),
        ],
        compiler_params=pltpu.CompilerParams(collective_id=0, has_side_effects=True),
    )(tokens, w_in, w_down, old_place, new_place, expert_ids, replica, combine)


def solution(mesh):
    placed = (
        P(("group", "expert"), None),
        P(None, None, ("group", "expert")),
        P(("group", "expert"), None),
        P("group"),
        P("group"),
        P(("group", "expert"), None),
        P(("group", "expert"), None),
        P(("group", "expert"), None),
    )
    return jax.shard_map(
        body, mesh=mesh, in_specs=placed, out_specs=P(("group", "expert"), None), check_vma=False
    )
```

time: 145 us -> 70.7 us (0.49)
  the two profiles are of different devices: /device:TPU:1 before, /device:TPU:8 now
where the time goes in v1:
time: 70.7 us; the launch traced here: 70.5 us
  Pallas kernels  64.9 us (92%)
  local copies, waits for them, and re-layouts  5.61 us (8%)
    pallas_call x1, Pallas kernels, body(): pl.pallas_call(kernel, out_shape=jax.ShapeDtypeStruct((count, width), BF1...  64.9 us
    unnamed x4, local copies, waits for them, and re-layouts  5.61 us

profile of v1, /device:TPU:8, one launch (start us, length us, event | category | flops | bytes accessed | tf_op | source)
XLA Modules:
  0.0 70.5 jit_solution(16456903903269013216)
XLA Ops:
  0.0 1.4 %copy.9.expert_ids = s32[16,2]{1,0:T(8,128)} copy(s32[16,2]{0,1:T(2,128)} %param.13) | data formatting | bytes 256 | tf_op args[5]
  1.4 1.4 %copy.10.replica = s32[16,2]{1,0:T(8,128)} copy(s32[16,2]{0,1:T(2,128)} %param.14) | data formatting | bytes 256 | tf_op args[6]
  2.7 1.3 %copy.11.combine = f32[16,2]{1,0:T(8,128)} copy(f32[16,2]{0,1:T(2,128)} %param.15) | data formatting | bytes 256 | tf_op args[7]
  4.1 64.9 %shard_map.82 = bf16[16,3584]{1,0:T(8,128)(2,1)} custom-call(bf16[16,3584]{1,0:T(8,128)(2,1)} %tokens.1, bf16[2,3584,128]{2,1,0:T(8,128)(2,1)} %w_in.1, bf16[128,3584]{1,0:T(8,128)(2,1)} %w_down.1, s32[8]{0:T(128)} %old_place.1, s32[8]{0:T(128)} %new_place.1, s32[16,2]{1,0:T(8,128)} %copy.9.expert_ids, s32[16,2]{1,0:T(8,128)} %copy.10.replica, ...), custom_call_target="tpu_custom_call" | custom-call | tf_op jit(solution)/shard_map/pallas_call | solution.py:261
  68.9 1.6 %copy.13 = bf16[16,3584]{1,0:T(8,128)(2,1)} copy(bf16[16,3584]{1,0:T(8,128)(2,1)} %shard_map.82) | data formatting | bytes 229376

commit v2 on v1

v2 whole, which is shorter than its diff:
```python
import jax
import jax.numpy as jnp
from jax import lax
from jax.experimental import pallas as pl
from jax.experimental.pallas import tpu as pltpu
from jax.sharding import PartitionSpec as P

SLOTS = 8
CAP = 4
NX, NY = 4, 8
META = 128
TILE = 512
F32 = jnp.float32
BF16 = jnp.bfloat16


def routing_meta(old_place, new_place, expert_ids, replica, combine):
    rows = expert_ids.shape[1]
    diagonal = (lax.broadcasted_iota(jnp.int32, (rows, rows), 0)
                == lax.broadcasted_iota(jnp.int32, (rows, rows), 1))

    def column_of(array, k):
        return jnp.sum(jnp.where(diagonal, array[k:k + 1, :], 0), axis=1, keepdims=True)

    lane = lax.broadcasted_iota(jnp.int32, (1, META), 1)
    new_vec = jnp.full((1, META), -1, jnp.int32)
    old_vec = jnp.full((1, META), -1, jnp.int32)
    for t in range(SLOTS):
        new_vec = jnp.where(lane == t, new_place[t], new_vec)
        old_vec = jnp.where(lane == t, old_place[t], old_vec)
    count = jnp.zeros((1, META), jnp.int32)
    rank = jnp.zeros((1, META), jnp.int32)
    for t in range(SLOTS):
        same = jnp.where(new_vec == new_place[t], 1, 0)
        count = count + same
        rank = rank + jnp.where(lane > t, same, 0)
    source = jnp.where(new_vec == old_vec, lane, lane + 1 - 2 * (lane & 1))
    chosen = []
    for k in range(2):
        wanted = column_of(replica, k)
        wanted = jnp.where(wanted < count, wanted, wanted - count)
        hit = (new_vec == column_of(expert_ids, k)) & (rank == wanted)
        chosen.append(jnp.where(hit, 1.0, 0.0))
    row_i = lax.broadcasted_iota(jnp.int32, (rows, rows), 0)
    col_i = lax.broadcasted_iota(jnp.int32, (rows, rows), 1)
    earlier = jnp.where(col_i < row_i, 1.0, 0.0).astype(BF16)
    before = jnp.dot(earlier, (chosen[0] + chosen[1]).astype(BF16), preferred_element_type=F32)
    lanes = lax.broadcasted_iota(jnp.int32, (rows, META), 1)
    column = (lanes & 31).astype(F32)
    block = lanes >> 5
    source_f = (source * CAP).astype(F32)
    meta = jnp.zeros((rows, META), F32)
    for k in range(2):
        ahead = before if k == 0 else before + chosen[0]
        position = jnp.sum(chosen[k] * ahead, axis=1, keepdims=True)
        target = jnp.sum(chosen[k] * source_f, axis=1, keepdims=True) + position
        weight = column_of(combine, k)
        high = weight.astype(BF16).astype(F32)
        middle = (weight - high).astype(BF16).astype(F32)
        low = weight - high - middle
        value = jnp.where(block == 0, high, jnp.where(block == 1, middle, jnp.where(block == 2, low, 1.0)))
        meta = meta + jnp.where((column == target) & (position < float(CAP)), value, 0.0)
    return meta.astype(BF16)


def kernel(tokens, w_in, w_down, old_place, new_place, expert_ids, replica, combine, out,
           units, sel, rows, w_gu, w_d, r_send, r_recv, part, y_send, y_recv, y_far,
           old_s, new_s, ids_v, rep_v, comb_v, ssem, rsem, wsem):
    width = tokens.shape[1]
    hid = w_down.shape[0]
    me = lax.axis_index("expert")
    core = me % 2
    y = (me // 2) % NY
    x = me // (2 * NY)
    half = y // (NY // 2)

    def device(xx, yy, cc):
        return {"expert": (xx * NY + yy) * 2 + cc}

    up, up2 = device(x, (y + 1) % NY, core), device(x, (y + 2) % NY, core)
    down, down2 = device(x, (y + NY - 1) % NY, core), device(x, (y + NY - 2) % NY, core)
    partner = device(x, y, 1 - core)
    right = [device((x + d) % NX, y, core) for d in range(NX)]
    left = [device((x + NX - d) % NX, y, core) for d in range(NX)]

    barrier = pltpu.get_barrier_semaphore()
    peers = [up, down, up2, down2, partner] + right[1:]
    for peer in peers:
        pl.semaphore_signal(barrier, inc=1, device_id=peer, device_id_type=pl.DeviceIdType.MESH)

    split = width // 2
    quarter = width // 4

    def local(i, src, dst):
        copy = pltpu.make_async_copy(src, dst, wsem.at[i])
        copy.start()
        return copy

    small = [local(i, src, dst) for i, (src, dst) in enumerate((
        (old_place, old_s), (new_place, new_s), (expert_ids, ids_v), (replica, rep_v), (combine, comb_v)))]
    own = [local(5, tokens.at[:, pl.ds(0, split)], units.at[0, :, pl.ds(0, split)]),
           local(6, tokens.at[:, pl.ds(split, split)], units.at[0, :, pl.ds(split + META, split)])]
    loads = [local(7, w_in.at[0], w_gu.at[:, 0:hid]), local(8, w_in.at[1], w_gu.at[:, 2 * hid:3 * hid]),
             local(9, w_down, w_d.at[0:hid])]

    sent = []

    def push(src, dst, target):
        i = len(sent)
        copy = pltpu.make_async_remote_copy(
            src_ref=src, dst_ref=dst, send_sem=ssem.at[i], recv_sem=rsem.at[i],
            device_id=target, device_id_type=pl.DeviceIdType.MESH)
        copy.start()
        sent.append(copy)
        return copy

    cuts = (pl.ds(0, quarter), pl.ds(quarter, quarter), pl.ds(split, META + quarter),
            pl.ds(split + META + quarter, quarter))
    parts = (slice(0, split), slice(split, width))
    places = (slice(0, split), slice(split + META, META + width))
    spots = slice(split, split + META)
    quarters = [slice(c * quarter, (c + 1) * quarter) for c in range(4)]
    cut_q = [pl.ds(c * quarter, quarter) for c in range(4)]
    cut_h = [pl.ds(h * split, split) for h in range(2)]

    def forward(src, dst, target, c):
        return push(units.at[src, :, cuts[c]], units.at[dst, :, cuts[c]], target)

    pl.semaphore_wait(barrier, len(peers))
    a1 = {}
    for c in (0, 1):
        piece = tokens.at[:, cut_q[c]]
        a1[c] = (push(piece, units.at[1, :, cuts[c]], up), push(piece, units.at[2, :, cuts[c]], down))
    w_peer = [push(w_in.at[0], w_gu.at[:, hid:2 * hid], partner),
              push(w_in.at[1], w_gu.at[:, 3 * hid:4 * hid], partner),
              push(w_down, w_d.at[hid:2 * hid], partner)]
    for copy in small:
        copy.wait()
    units[0, :, spots] = routing_meta(old_s, new_s, ids_v[...], rep_v[...], comb_v[...])
    own[1].wait()
    a1[2] = (forward(0, 1, up, 2), forward(0, 2, down, 2))
    piece = tokens.at[:, cut_q[3]]
    a1[3] = (push(piece, units.at[1, :, cuts[3]], up), push(piece, units.at[2, :, cuts[3]], down))
    a2 = []
    for c in range(4):
        a1[c][0].wait_recv()
        u = forward(1, 3, up, c)
        a1[c][1].wait_recv()
        a2.append((u, forward(2, 4, down, c)))
    a3, a4 = [], []
    for c in range(4):
        a2[c][0].wait_recv()
        u = forward(3, 5, up, c)
        if c % 2 == 0:
            a4.append(forward(3, 7, up2, c))
        a2[c][1].wait_recv()
        a3.append((u, forward(4, 6, down, c)))
        if c % 2 == 1:
            a4.append(forward(4, 7, down2, c))

    def wanted_by(n, block):
        return 32 * block + 8 * ((x + (n >> 4)) & (NX - 1)) + CAP * half + (n & 3)

    lane_i = lax.broadcasted_iota(jnp.int32, (META, 3 * META), 0)
    n_i = lax.broadcasted_iota(jnp.int32, (META, 3 * META), 1)
    n_in = n_i & (META - 1)
    spread = jnp.where((lane_i == wanted_by(n_in, n_i >> 7)) & (n_in < 64), 1.0, 0.0).astype(BF16)
    n_t = lax.broadcasted_iota(jnp.int32, (64, META), 0)
    spread_t = jnp.where(lax.broadcasted_iota(jnp.int32, (64, META), 1) == wanted_by(n_t, 3), 1.0, 0.0).astype(BF16)
    i_row = lax.broadcasted_iota(jnp.int32, (64, 64), 0)
    i_col = lax.broadcasted_iota(jnp.int32, (64, 64), 1)
    same_unit = (i_row >> 4) == ((i_col >> 2) & 3)
    same_unit_t = (i_col >> 4) == ((i_row >> 2) & 3)

    def weights_of(g):
        meta = units[4 * g:4 * g + 4, :, spots].reshape(64, META)
        picks = jnp.dot(meta, spread, preferred_element_type=F32)
        return jnp.concatenate(
            [jnp.where(same_unit, picks[:, q * META:q * META + 64], 0.0).astype(BF16) for q in range(3)], axis=0)

    def select(g):
        meta = units[4 * g:4 * g + 4, :, spots].reshape(64, META)
        picks = lax.dot_general(spread_t, meta, (((1,), (1,)), ((), ())), preferred_element_type=F32)
        picks = jnp.where(same_unit_t, picks, 0.0).astype(BF16)
        copies = []
        for h in range(2):
            for j in range(7):
                at = h * (split + META) + j * 256
                cut = slice(h * split + j * 256, h * split + (j + 1) * 256)
                group = units[4 * g:4 * g + 4, :, at:at + 256].reshape(64, 256)
                got = jnp.dot(picks, group, preferred_element_type=F32)
                got = got.astype(BF16)
                rows[g, 0, :, cut] = got[0:16]
                for d in range(1, NX):
                    sel[g, d, :, cut] = got[16 * d:16 * d + 16]
            copies.append({d: push(sel.at[g, d, :, cut_h[h]], rows.at[g, d, :, cut_h[h]], right[d])
                           for d in (2, 1, 3)})
        return copies

    def experts(g, copies):
        gate_up = jnp.zeros((64, 4 * hid), F32)
        for h in range(2):
            for d in (1, 3, 2):
                copies[h][d].wait_recv()
            block = rows[g, :, :, parts[h]].reshape(64, split)
            gate_up = gate_up + jnp.dot(block, w_gu[parts[h], :], preferred_element_type=F32)
        gate = gate_up[:, :2 * hid]
        hidden = (gate * jax.nn.sigmoid(gate) * gate_up[:, 2 * hid:]).astype(BF16)
        back = []
        for h in range(2):
            for j in range(7):
                cut = slice(h * split + j * 256, h * split + (j + 1) * 256)
                value = jnp.dot(hidden, w_d[:, cut], preferred_element_type=F32).astype(BF16)
                r_recv[g, 0:16, cut] = value[0:16]
                r_send[g, 16:64, cut] = value[16:64]
            back.append([push(r_send.at[g, pl.ds(16 * d, 16), cut_h[h]], r_recv.at[g, pl.ds(16 * d, 16), cut_h[h]],
                              left[d]) for d in (2, 1, 3)])
        return back

    def mix(g, h, weights, copies):
        for copy in copies:
            copy.wait_recv()
        for j in range(7):
            cut = slice(h * split + j * 256, h * split + (j + 1) * 256)
            value = jnp.dot(weights, r_recv[g, :, cut], preferred_element_type=F32)
            value = value[0:64] + value[64:128] + value[128:192]
            part[4 * g:4 * g + 4, :, cut] = value.reshape(4, 16, 256)

    def hand(k, dst, c, target, *arrived):
        value = part[k, :, quarters[c]]
        for copy, buffer in arrived:
            copy.wait_recv()
            value = value + buffer[:, quarters[c]].astype(F32)
        y_send[k, :, quarters[c]] = value.astype(BF16)
        return push(y_send.at[k, :, cut_q[c]], dst.at[:, cut_q[c]], target)

    own[0].wait()
    x_a = select(0)
    for c in range(4):
        a3[c][0].wait_recv()
        a3[c][1].wait_recv()
    for copy in a4:
        copy.wait_recv()
    x_b = select(1)
    for load in loads:
        load.wait()
    for copy in w_peer:
        copy.wait_recv()
    r_a = experts(0, x_a)
    r_b = experts(1, x_b)
    weights_a, weights_b = weights_of(0), weights_of(1)
    for h in range(2):
        mix(0, h, weights_a, r_a[h])
    far_down, far_up, go_down, go_up = {}, {}, {}, {}
    for h in range(2):
        mix(1, h, weights_b, r_b[h])
        even, odd = 2 * h, 2 * h + 1
        far_down[even] = hand(7, y_far.at[0], even, down2)
        far_up[odd] = hand(7, y_far.at[1], odd, up2)
        for c in (odd, even):
            go_down[c] = hand(5, y_recv.at[3], c, down)
        for c in (even, odd):
            go_up[c] = hand(6, y_recv.at[4], c, up)
    order = ((1, 0), (3, 2), (0, 1), (2, 3))
    for c_down, c_up in order:
        extra = ((far_down[c_down], y_far.at[0]),) if c_down in far_down else ()
        go_down[c_down] = hand(3, y_recv.at[1], c_down, down, (go_down[c_down], y_recv.at[3]), *extra)
        extra = ((far_up[c_up], y_far.at[1]),) if c_up in far_up else ()
        go_up[c_up] = hand(4, y_recv.at[2], c_up, up, (go_up[c_up], y_recv.at[4]), *extra)
    for c_down, c_up in order:
        go_down[c_down] = hand(1, y_recv.at[0], c_down, down, (go_down[c_down], y_recv.at[1]))
        go_up[c_up] = hand(2, y_recv.at[7], c_up, up, (go_up[c_up], y_recv.at[2]))
    for c in (1, 3, 0, 2):
        go_down[c].wait_recv()
        go_up[c].wait_recv()
        value = (part[0, :, quarters[c]] + y_recv[0, :, quarters[c]].astype(F32)
                 + y_recv[7, :, quarters[c]].astype(F32))
        out[:, quarters[c]] = value.astype(BF16)
    for copy in sent:
        copy.wait_send()


COPIES = 28 + 3 + 12 + 12 + 28


def body(tokens, w_in, w_down, old_place, new_place, expert_ids, replica, combine):
    count, width = tokens.shape
    hid = w_down.shape[0]
    vmem = pl.BlockSpec(memory_space=pltpu.VMEM)
    hbm = pl.BlockSpec(memory_space=pl.ANY)
    return pl.pallas_call(
        kernel,
        out_shape=jax.ShapeDtypeStruct((count, width), BF16),
        in_specs=[hbm] * 8,
        out_specs=vmem,
        scratch_shapes=[
            pltpu.VMEM((8, count, META + width), BF16),
            pltpu.VMEM((2, NX, 16, width), BF16),
            pltpu.VMEM((2, NX, 16, width), BF16),
            pltpu.VMEM((width, 4 * hid), BF16),
            pltpu.VMEM((2 * hid, width), BF16),
            pltpu.VMEM((2, 64, width), BF16),
            pltpu.VMEM((2, 64, width), BF16),
            pltpu.VMEM((8, count, width), F32),
            pltpu.VMEM((8, count, width), BF16),
            pltpu.VMEM((8, count, width), BF16),
            pltpu.VMEM((2, count, width), BF16),
            pltpu.SMEM((SLOTS,), jnp.int32),
            pltpu.SMEM((SLOTS,), jnp.int32),
            pltpu.VMEM((2, count), jnp.int32),
            pltpu.VMEM((2, count), jnp.int32),
            pltpu.VMEM((2, count), F32),
            pltpu.SemaphoreType.DMA((COPIES,)),
            pltpu.SemaphoreType.DMA((COPIES,)),
            pltpu.SemaphoreType.DMA((10,)),
        ],
        compiler_params=pltpu.CompilerParams(collective_id=0, has_side_effects=True),
    )(tokens, w_in, w_down, old_place, new_place, expert_ids.T, replica.T, combine.T)


def solution(mesh):
    placed = (
        P(("group", "expert"), None),
        P(None, None, ("group", "expert")),
        P(("group", "expert"), None),
        P("group"),
        P("group"),
        P(("group", "expert"), None),
        P(("group", "expert"), None),
        P(("group", "expert"), None),
    )
    return jax.shard_map(
        body, mesh=mesh, in_specs=placed, out_specs=P(("group", "expert"), None), check_vma=False
    )
```

time: 70.7 us -> 60.2 us (0.85)
  the two profiles are of different devices: /device:TPU:8 before, /device:TPU:2 now
where the time goes in v2:
time: 60.2 us; the launch traced here: 60.1 us
  Pallas kernels  58.5 us (97%)
  local copies, waits for them, and re-layouts  1.55 us (3%)
    pallas_call x1, Pallas kernels, body(): pl.pallas_call(kernel, out_shape=jax.ShapeDtypeStruct((count, width), BF1...  58.5 us
    unnamed x1, local copies, waits for them, and re-layouts  1.55 us

profile of v2, /device:TPU:2, one launch (start us, length us, event | category | flops | bytes accessed | tf_op | source)
XLA Modules:
  0.0 60.1 jit_solution(2383738489296900694)
XLA Ops:
  0.0 58.5 %shard_map.82 = bf16[16,3584]{1,0:T(8,128)(2,1)} custom-call(bf16[16,3584]{1,0:T(8,128)(2,1)} %tokens.1, bf16[2,3584,128]{2,1,0:T(8,128)(2,1)} %w_in.1, bf16[128,3584]{1,0:T(8,128)(2,1)} %w_down.1, s32[8]{0:T(128)} %old_place.1, s32[8]{0:T(128)} %new_place.1, s32[2,16]{1,0:T(2,128)} %bitcast.3, s32[2,16]{1,0:T(2,128)} %bitcast.4, f32[2,16]{1,0:T(2,128)} %bitcast.5), custom_call_target="tpu_custom_call" | custom-call | tf_op jit(solution)/shard_map/pallas_call | solution.py:291
  58.5 1.6 %copy.10 = bf16[16,3584]{1,0:T(8,128)(2,1)} copy(bf16[16,3584]{1,0:T(8,128)(2,1)} %shard_map.82) | data formatting | bytes 229376

commit v3 on v2

--- a/solution.py
+++ b/solution.py
@@ -65,7 +65,7 @@
 
 def kernel(tokens, w_in, w_down, old_place, new_place, expert_ids, replica, combine, out,
            units, sel, rows, w_gu, w_d, r_send, r_recv, part, y_send, y_recv, y_far,
-           old_s, new_s, ids_v, rep_v, comb_v, ssem, rsem, wsem):
+           old_s, new_s, ids_v, rep_v, comb_v, out_v, ssem, rsem, wsem):
     width = tokens.shape[1]
     hid = w_down.shape[0]
     me = lax.axis_index("expert")
@@ -98,12 +98,11 @@
 
     small = [local(i, src, dst) for i, (src, dst) in enumerate((
         (old_place, old_s), (new_place, new_s), (expert_ids, ids_v), (replica, rep_v), (combine, comb_v)))]
-    own = [local(5, tokens.at[:, pl.ds(0, split)], units.at[0, :, pl.ds(0, split)]),
-           local(6, tokens.at[:, pl.ds(split, split)], units.at[0, :, pl.ds(split + META, split)])]
-    loads = [local(7, w_in.at[0], w_gu.at[:, 0:hid]), local(8, w_in.at[1], w_gu.at[:, 2 * hid:3 * hid]),
-             local(9, w_down, w_d.at[0:hid])]
-
-    sent = []
+    own = local(5, tokens, units.at[0, :, pl.ds(META, width)])
+    loads = [local(6, w_in.at[0], w_gu.at[:, 0:hid]), local(7, w_in.at[1], w_gu.at[:, 2 * hid:3 * hid]),
+             local(8, w_down, w_d.at[0:hid])]
+
+    sent, cleared = [], []
 
     def push(src, dst, target):
         i = len(sent)
@@ -114,11 +113,9 @@
         sent.append(copy)
         return copy
 
-    cuts = (pl.ds(0, quarter), pl.ds(quarter, quarter), pl.ds(split, META + quarter),
-            pl.ds(split + META + quarter, quarter))
+    cuts = (pl.ds(0, META + quarter),) + tuple(pl.ds(META + c * quarter, quarter) for c in (1, 2, 3))
     parts = (slice(0, split), slice(split, width))
-    places = (slice(0, split), slice(split + META, META + width))
-    spots = slice(split, split + META)
+    spots = slice(0, META)
     quarters = [slice(c * quarter, (c + 1) * quarter) for c in range(4)]
     cut_q = [pl.ds(c * quarter, quarter) for c in range(4)]
     cut_h = [pl.ds(h * split, split) for h in range(2)]
@@ -127,36 +124,38 @@
         return push(units.at[src, :, cuts[c]], units.at[dst, :, cuts[c]], target)
 
     pl.semaphore_wait(barrier, len(peers))
-    a1 = {}
-    for c in (0, 1):
+    chunks = (1, 0, 2, 3)
+    a1, a2, a3, far = {}, {}, {}, {}
+
+    def first(c):
         piece = tokens.at[:, cut_q[c]]
         a1[c] = (push(piece, units.at[1, :, cuts[c]], up), push(piece, units.at[2, :, cuts[c]], down))
+
+    first(1)
     w_peer = [push(w_in.at[0], w_gu.at[:, hid:2 * hid], partner),
               push(w_in.at[1], w_gu.at[:, 3 * hid:4 * hid], partner),
               push(w_down, w_d.at[hid:2 * hid], partner)]
     for copy in small:
         copy.wait()
     units[0, :, spots] = routing_meta(old_s, new_s, ids_v[...], rep_v[...], comb_v[...])
-    own[1].wait()
-    a1[2] = (forward(0, 1, up, 2), forward(0, 2, down, 2))
-    piece = tokens.at[:, cut_q[3]]
-    a1[3] = (push(piece, units.at[1, :, cuts[3]], up), push(piece, units.at[2, :, cuts[3]], down))
-    a2 = []
-    for c in range(4):
+    own.wait()
+    a1[0] = (forward(0, 1, up, 0), forward(0, 2, down, 0))
+    first(2)
+    first(3)
+    for c in chunks:
         a1[c][0].wait_recv()
         u = forward(1, 3, up, c)
         a1[c][1].wait_recv()
-        a2.append((u, forward(2, 4, down, c)))
-    a3, a4 = [], []
-    for c in range(4):
+        a2[c] = (u, forward(2, 4, down, c))
+    for c in chunks:
         a2[c][0].wait_recv()
         u = forward(3, 5, up, c)
         if c % 2 == 0:
-            a4.append(forward(3, 7, up2, c))
+            far[c] = forward(3, 7, up2, c)
         a2[c][1].wait_recv()
-        a3.append((u, forward(4, 6, down, c)))
+        a3[c] = (u, forward(4, 6, down, c))
         if c % 2 == 1:
-            a4.append(forward(4, 7, down2, c))
+            far[c] = forward(4, 7, down2, c)
 
     def wanted_by(n, block):
         return 32 * block + 8 * ((x + (n >> 4)) & (NX - 1)) + CAP * half + (n & 3)
@@ -178,14 +177,17 @@
         return jnp.concatenate(
             [jnp.where(same_unit, picks[:, q * META:q * META + 64], 0.0).astype(BF16) for q in range(3)], axis=0)
 
-    def select(g):
-        meta = units[4 * g:4 * g + 4, :, spots].reshape(64, META)
-        picks = lax.dot_general(spread_t, meta, (((1,), (1,)), ((), ())), preferred_element_type=F32)
-        picks = jnp.where(same_unit_t, picks, 0.0).astype(BF16)
+    def select(g, ready):
         copies = []
         for h in range(2):
+            for copy in ready[h]:
+                copy.wait_recv()
+            if h == 0:
+                meta = units[4 * g:4 * g + 4, :, spots].reshape(64, META)
+                picks = lax.dot_general(spread_t, meta, (((1,), (1,)), ((), ())), preferred_element_type=F32)
+                picks = jnp.where(same_unit_t, picks, 0.0).astype(BF16)
             for j in range(7):
-                at = h * (split + META) + j * 256
+                at = META + h * split + j * 256
                 cut = slice(h * split + j * 256, h * split + (j + 1) * 256)
                 group = units[4 * g:4 * g + 4, :, at:at + 256].reshape(64, 256)
                 got = jnp.dot(picks, group, preferred_element_type=F32)
@@ -197,7 +199,7 @@
                            for d in (2, 1, 3)})
         return copies
 
-    def experts(g, copies):
+    def experts(g, copies, clear):
         gate_up = jnp.zeros((64, 4 * hid), F32)
         for h in range(2):
             for d in (1, 3, 2):
@@ -213,6 +215,10 @@
                 value = jnp.dot(hidden, w_d[:, cut], preferred_element_type=F32).astype(BF16)
                 r_recv[g, 0:16, cut] = value[0:16]
                 r_send[g, 16:64, cut] = value[16:64]
+            for d in (1, 2, 3):
+                if clear is not None:
+                    clear[h][d].wait_send()
+                    cleared.append(clear[h][d])
             back.append([push(r_send.at[g, pl.ds(16 * d, 16), cut_h[h]], r_recv.at[g, pl.ds(16 * d, 16), cut_h[h]],
                               left[d]) for d in (2, 1, 3)])
         return back
@@ -234,23 +240,16 @@
         y_send[k, :, quarters[c]] = value.astype(BF16)
         return push(y_send.at[k, :, cut_q[c]], dst.at[:, cut_q[c]], target)
 
-    own[0].wait()
-    x_a = select(0)
-    for c in range(4):
-        a3[c][0].wait_recv()
-        a3[c][1].wait_recv()
-    for copy in a4:
-        copy.wait_recv()
-    x_b = select(1)
+    x_a = select(0, ((), ()))
+    x_b = select(1, [[a3[c][0] for c in cs] + [a3[c][1] for c in cs] + [far[c] for c in cs]
+                     for cs in ((1, 0), (2, 3))])
     for load in loads:
         load.wait()
     for copy in w_peer:
         copy.wait_recv()
-    r_a = experts(0, x_a)
-    r_b = experts(1, x_b)
+    r_a = experts(0, x_a, x_b)
+    r_b = experts(1, x_b, None)
     weights_a, weights_b = weights_of(0), weights_of(1)
-    for h in range(2):
-        mix(0, h, weights_a, r_a[h])
     far_down, far_up, go_down, go_up = {}, {}, {}, {}
     for h in range(2):
         mix(1, h, weights_b, r_b[h])
@@ -261,6 +260,8 @@
             go_down[c] = hand(5, y_recv.at[3], c, down)
         for c in (even, odd):
             go_up[c] = hand(6, y_recv.at[4], c, up)
+    for h in range(2):
+        mix(0, h, weights_a, r_a[h])
     order = ((1, 0), (3, 2), (0, 1), (2, 3))
     for c_down, c_up in order:
         extra = ((far_down[c_down], y_far.at[0]),) if c_down in far_down else ()
@@ -270,14 +271,19 @@
     for c_down, c_up in order:
         go_down[c_down] = hand(1, y_recv.at[0], c_down, down, (go_down[c_down], y_recv.at[1]))
         go_up[c_up] = hand(2, y_recv.at[7], c_up, up, (go_up[c_up], y_recv.at[2]))
+    done = []
     for c in (1, 3, 0, 2):
         go_down[c].wait_recv()
         go_up[c].wait_recv()
         value = (part[0, :, quarters[c]] + y_recv[0, :, quarters[c]].astype(F32)
                  + y_recv[7, :, quarters[c]].astype(F32))
-        out[:, quarters[c]] = value.astype(BF16)
+        out_v[:, quarters[c]] = value.astype(BF16)
+        done.append(local(9 + c, out_v.at[:, cut_q[c]], out.at[:, cut_q[c]]))
     for copy in sent:
-        copy.wait_send()
+        if not any(copy is other for other in cleared):
+            copy.wait_send()
+    for copy in done:
+        copy.wait()
 
 
 COPIES = 28 + 3 + 12 + 12 + 28
@@ -286,13 +292,12 @@
 def body(tokens, w_in, w_down, old_place, new_place, expert_ids, replica, combine):
     count, width = tokens.shape
     hid = w_down.shape[0]
-    vmem = pl.BlockSpec(memory_space=pltpu.VMEM)
     hbm = pl.BlockSpec(memory_space=pl.ANY)
     return pl.pallas_call(
         kernel,
         out_shape=jax.ShapeDtypeStruct((count, width), BF16),
-        in_specs=[hbm] * 8,
-        out_specs=vmem,
+        in_specs=[pl.BlockSpec(memory_space=pltpu.MemorySpace.HBM)] * 8,
+        out_specs=hbm,
         scratch_shapes=[
             pltpu.VMEM((8, count, META + width), BF16),
             pltpu.VMEM((2, NX, 16, width), BF16),
@@ -310,12 +315,15 @@
             pltpu.VMEM((2, count), jnp.int32),
             pltpu.VMEM((2, count), jnp.int32),
             pltpu.VMEM((2, count), F32),
+            pltpu.VMEM((count, width), BF16),
             pltpu.SemaphoreType.DMA((COPIES,)),
             pltpu.SemaphoreType.DMA((COPIES,)),
-            pltpu.SemaphoreType.DMA((10,)),
+            pltpu.SemaphoreType.DMA((13,)),
         ],
-        compiler_params=pltpu.CompilerParams(collective_id=0, has_side_effects=True),
-    )(tokens, w_in, w_down, old_place, new_place, expert_ids.T, replica.T, combine.T)
+        compiler_params=pltpu.CompilerParams(
+            collective_id=0, has_side_effects=True, vmem_limit_bytes=32 << 20),
+    )(*[pltpu.with_memory_space_constraint(a, pltpu.MemorySpace.HBM) for a in (
+        tokens, w_in, w_down, old_place, new_place, expert_ids.T, replica.T, combine.T)])
 
 
 def solution(mesh):

time: 60.2 us -> 58.5 us (0.972)
  local copies, waits for them, and re-layouts: 1.55 us -> 0.65 us
  Pallas kernels: 58.5 us -> 57.7 us
    unnamed x1, local copies, waits for them, and re-layouts: 1.55 us -> 0.65 us
    pallas_call x1, Pallas kernels: 58.5 us -> 57.7 us  [body(): pl.pallas_call(kernel, out_shape=jax.ShapeDtypeStruct((count, width), BF1...]
where the time goes in v3:
time: 58.5 us; the launch traced here: 58.3 us
  Pallas kernels  57.7 us (99%)
  local copies, waits for them, and re-layouts  0.65 us (1%)
    pallas_call x1, Pallas kernels, body(): pl.pallas_call(kernel, out_shape=jax.ShapeDtypeStruct((count, width), BF1...  57.7 us

profile of v3, /device:TPU:2, one launch (start us, length us, event | category | flops | bytes accessed | tf_op | source)
XLA Modules:
  0.0 58.3 jit_solution(3830340052473334257)
XLA Ops:
  0.0 57.7 %shard_map.82 = bf16[16,3584]{1,0:T(8,128)(2,1)S(1)} custom-call(bf16[16,3584]{1,0:T(8,128)(2,1)} %tokens.1, bf16[2,3584,128]{2,1,0:T(8,128)(2,1)} %w_in.1, bf16[128,3584]{1,0:T(8,128)(2,1)} %w_down.1, s32[8]{0:T(128)} %old_place.1, s32[8]{0:T(128)} %new_place.1, s32[2,16]{1,0:T(2,128)} %bitcast.3, s32[2,16]{1,0:T(2,128)} %bitcast.4, f32[2,16]{1,0:T(2,128)} %bitcast.5), custom_call_target="tpu_custom_call" | custom-call | tf_op jit(solution)/shard_map/pallas_call | solution.py:296
  57.7 0.6 %copy.10 = bf16[16,3584]{1,0:T(8,128)(2,1)} copy(bf16[16,3584]{1,0:T(8,128)(2,1)S(1)} %shard_map.82) | data formatting | bytes 229376

commit v4 on v3

--- a/solution.py
+++ b/solution.py
@@ -102,7 +102,7 @@
     loads = [local(6, w_in.at[0], w_gu.at[:, 0:hid]), local(7, w_in.at[1], w_gu.at[:, 2 * hid:3 * hid]),
              local(8, w_down, w_d.at[0:hid])]
 
-    sent, cleared = [], []
+    sent = []
 
     def push(src, dst, target):
         i = len(sent)
@@ -199,7 +199,11 @@
                            for d in (2, 1, 3)})
         return copies
 
-    def experts(g, copies, clear):
+    def give_back(g, h):
+        return [push(r_send.at[g, pl.ds(16 * d, 16), cut_h[h]], r_recv.at[g, pl.ds(16 * d, 16), cut_h[h]], left[d])
+                for d in (2, 1, 3)]
+
+    def experts(g, copies, at_once):
         gate_up = jnp.zeros((64, 4 * hid), F32)
         for h in range(2):
             for d in (1, 3, 2):
@@ -215,12 +219,8 @@
                 value = jnp.dot(hidden, w_d[:, cut], preferred_element_type=F32).astype(BF16)
                 r_recv[g, 0:16, cut] = value[0:16]
                 r_send[g, 16:64, cut] = value[16:64]
-            for d in (1, 2, 3):
-                if clear is not None:
-                    clear[h][d].wait_send()
-                    cleared.append(clear[h][d])
-            back.append([push(r_send.at[g, pl.ds(16 * d, 16), cut_h[h]], r_recv.at[g, pl.ds(16 * d, 16), cut_h[h]],
-                              left[d]) for d in (2, 1, 3)])
+            if at_once:
+                back.append(give_back(g, h))
         return back
 
     def mix(g, h, weights, copies):
@@ -247,8 +247,9 @@
         load.wait()
     for copy in w_peer:
         copy.wait_recv()
-    r_a = experts(0, x_a, x_b)
-    r_b = experts(1, x_b, None)
+    experts(0, x_a, False)
+    r_b = experts(1, x_b, True)
+    r_a = [give_back(0, h) for h in range(2)]
     weights_a, weights_b = weights_of(0), weights_of(1)
     far_down, far_up, go_down, go_up = {}, {}, {}, {}
     for h in range(2):
@@ -280,8 +281,7 @@
         out_v[:, quarters[c]] = value.astype(BF16)
         done.append(local(9 + c, out_v.at[:, cut_q[c]], out.at[:, cut_q[c]]))
     for copy in sent:
-        if not any(copy is other for other in cleared):
-            copy.wait_send()
+        copy.wait_send()
     for copy in done:
         copy.wait()
 

time: 58.5 us -> 57.3 us (0.979)
  the two profiles are of different devices: /device:TPU:2 before, /device:TPU:6 now
where the time goes in v4:
time: 57.3 us; the launch traced here: 57.2 us
  Pallas kernels  56.5 us (99%)
  local copies, waits for them, and re-layouts  0.65 us (1%)
    pallas_call x1, Pallas kernels, body(): pl.pallas_call(kernel, out_shape=jax.ShapeDtypeStruct((count, width), BF1...  56.5 us

profile of v4, /device:TPU:6, one launch (start us, length us, event | category | flops | bytes accessed | tf_op | source)
XLA Modules:
  0.0 57.2 jit_solution(15543515232072486504)
XLA Ops:
  0.0 56.5 %shard_map.82 = bf16[16,3584]{1,0:T(8,128)(2,1)S(1)} custom-call(bf16[16,3584]{1,0:T(8,128)(2,1)} %tokens.1, bf16[2,3584,128]{2,1,0:T(8,128)(2,1)} %w_in.1, bf16[128,3584]{1,0:T(8,128)(2,1)} %w_down.1, s32[8]{0:T(128)} %old_place.1, s32[8]{0:T(128)} %new_place.1, s32[2,16]{1,0:T(2,128)} %bitcast.3, s32[2,16]{1,0:T(2,128)} %bitcast.4, f32[2,16]{1,0:T(2,128)} %bitcast.5), custom_call_target="tpu_custom_call" | custom-call | tf_op jit(solution)/shard_map/pallas_call | solution.py:296
  56.5 0.6 %copy.10 = bf16[16,3584]{1,0:T(8,128)(2,1)} copy(bf16[16,3584]{1,0:T(8,128)(2,1)S(1)} %shard_map.82) | data formatting | bytes 229376
